TPU v7x, 32 devices: a whole 2x2x4 slice. The times are simulated.
32 devices in a mesh: rows: 8 (over y, x, core), sub: 4 (over z).
Axes of the slice: x: 2, y: 2, z: 4, core: 2. Of those that a mesh axis runs over, the one named last changes fastest.
Arguments:
- old_basis: bfloat16 [32, 524288], P(None, ('rows', 'sub')), may hold values from -1 to 1
- snapshots: bfloat16 [512, 524288], P(None, ('rows', 'sub')), may hold values from -16 to 16
- gap_flags: int32 [512, 4096], P(None, ('rows', 'sub')), may hold values from 0 to 1, as said below
- sketch_seed: int32 [512, 64], replicated, may hold values from -1 to 1
Outputs:
- new_basis: float32 [32, 524288], P(None, ('rows', 'sub'))
- coefficients: float32 [32, 512], replicated
Inputs may be any that keep to these rules, and one draw needn't show every extreme that they name: `gap_flags`: 1 marks a block of 128 velocity rows measured in that snapshot, 0 a gap; every snapshot has measured blocks and gaps.
All inputs are finite; a program needn't handle non-finite values.
Results may differ from a plain program's by a relative error of at most 0.00135.
The roundings to bfloat16 on the way count: a program that leaves them out, or rounds other values in their place, can miss the bound.
Values may be sent and summed in bfloat16 or wider, within the bound.
No kernel may reach another device: no remote copies, remote signals or barrier semaphores. Data moves between devices by JAX's collectives and lax.ppermute only.
A program may use at most 192 MiB of HBM per device.

v0:
```python
import math
import jax
import jax.numpy as jnp
from jax import lax
from jax.sharding import PartitionSpec as P

POWER = 2
damping = 0.005
highest = lax.Precision.HIGHEST


def cholesky_last(system):
    extent = system.shape[0]
    factor = jnp.zeros_like(system)
    for column in range(extent):
        partial_sum = jnp.sum(factor * factor[column : column + 1], axis=1)
        remain = system[:, column] - partial_sum
        diagonal_root = jnp.sqrt(remain[column])
        lower_part = (jnp.arange(extent) >= column).reshape((extent,) + (1,) * (system.ndim - 2))
        factor = factor.at[:, column].set(jnp.where(lower_part, remain / diagonal_root, 0.0))
    return factor


def lower_solve(factor, target):
    extent = factor.shape[0]
    result = jnp.zeros_like(target)
    for column in range(extent):
        current = (target[column] - jnp.sum(factor[column] * result, axis=0)) / factor[
            column, column
        ]
        result = result.at[column].set(current)
    return result


def upper_solve(factor, target):
    extent = factor.shape[0]
    result = jnp.zeros_like(target)
    for column in reversed(range(extent)):
        current = (target[column] - jnp.sum(factor[:, column] * result, axis=0)) / factor[
            column, column
        ]
        result = result.at[column].set(current)
    return result


def solve_normal(grams, right, modes, rows_all):
    snapshot_count = grams.shape[0]
    identity = jnp.eye(modes, dtype=jnp.float32)[:, :, None]
    system = grams.T.reshape(modes, modes, snapshot_count) + damping * rows_all * identity
    factor = cholesky_last(system)
    return upper_solve(factor, lower_solve(factor, right.T))


def inverse_factor(products):
    extent = products.shape[0]
    factor = cholesky_last(products[:, :, None])
    return lower_solve(factor, jnp.eye(extent, dtype=jnp.float32))


def mask_blocks(samples, flag_blocks):
    snapshot_count, blocks_dev = flag_blocks.shape
    weights = flag_blocks.astype(samples.dtype)[:, :, None]
    return (samples.reshape(snapshot_count, blocks_dev, -1) * weights).reshape(snapshot_count, -1)


def refill(samples, flag_blocks, recon_low):
    snapshot_count, blocks_dev = flag_blocks.shape
    observed = (flag_blocks > 0)[:, :, None]
    combined = jnp.where(
        observed,
        samples.reshape(snapshot_count, blocks_dev, -1),
        recon_low.reshape(snapshot_count, blocks_dev, -1),
    )
    return combined.reshape(snapshot_count, -1)


def contract_rows(former, latter):
    return lax.dot_general(
        former, latter, (((1,), (1,)), ((), ())), preferred_element_type=jnp.float32
    )


def contract_first(former, latter):
    return lax.dot_general(
        former, latter, (((0,), (0,)), ((), ())), preferred_element_type=jnp.float32
    )


def per_device(old_basis, snapshots, gap_flags, sketch_seed):
    modes = old_basis.shape[0]
    rows_all = old_basis.shape[1] * lax.axis_size(("rows", "sub"))
    blocks_dev = gap_flags.shape[1]
    masked = mask_blocks(snapshots, gap_flags)
    right = contract_rows(masked, old_basis)
    pieces = old_basis.reshape(modes, blocks_dev, -1)
    block_grams = jnp.einsum("kbi,lbi->bkl", pieces, pieces, preferred_element_type=jnp.float32)
    block_rows = block_grams.reshape(blocks_dev, modes * modes)
    grams = jnp.dot(gap_flags.astype(jnp.float32), block_rows, precision=highest)
    mixer = sketch_seed.astype(jnp.bfloat16)
    gram_total, right_total = lax.psum((grams, right), ("rows", "sub"))
    coefficients = solve_normal(gram_total, right_total, modes, rows_all)
    recon_low = contract_first(coefficients.astype(jnp.bfloat16), old_basis).astype(jnp.bfloat16)
    filled = refill(snapshots, gap_flags, recon_low)
    sketch = contract_first(mixer, filled)
    inverse = None
    for sweep_index in range(POWER + 1):
        if sweep_index > 0:
            sketch = contract_first(mixer, filled)
        local_gram = lax.dot_general(
            sketch,
            sketch,
            (((1,), (1,)), ((), ())),
            precision=highest,
            preferred_element_type=jnp.float32,
        )
        products = lax.psum(local_gram, ("rows", "sub"))
        inverse = inverse_factor(products)
        if sweep_index < POWER:
            ortho_rows = jnp.dot(inverse, sketch, precision=highest).astype(jnp.bfloat16)
            mixer_share = lax.psum_scatter(
                contract_rows(filled, ortho_rows), ("rows", "sub"), scatter_dimension=0, tiled=True
            ).astype(jnp.bfloat16)
            mixer = lax.all_gather(mixer_share, ("rows", "sub"), axis=0, tiled=True)
    root_rows = math.sqrt(rows_all)
    new_basis = jnp.dot(inverse[:modes], sketch, precision=highest) * root_rows
    return (new_basis, coefficients)


def solution(mesh):
    in_specs = (P(None, ("rows", "sub")), P(None, ("rows", "sub")), P(None, ("rows", "sub")), P())
    out_specs = (P(None, ("rows", "sub")), P())
    return jax.shard_map(
        per_device, mesh=mesh, in_specs=in_specs, out_specs=out_specs, check_vma=False
    )
```

profile of v0, /device:TPU:0, one launch (start us, length us, event | category | flops | bytes accessed | tf_op | source)
XLA Modules:
  0.0 1549.7 jit_solution(17264317991794373059)
XLA Ops:
  9.1 2.1 copy.518
  11.2 2.8 fusion.6
  14.1 2.5 copy.519
  16.6 13.0 mul.4308
  29.6 24.4 %fusion.2 = f32[32,512]{1,0:T(8,128)} fusion(bf16[32,16384]{1,0:T(8,128)(2,1)S(1)} %copy-done, bf16[512,16384]{1,0:T(8,128)(2,1)} %param.965, bf16[64,8,128,128]{3,2,1,0:T(8,128)(2,1)} %bitcast.3922), kind=kOutput, calls=%fused_computation.40 | convolution fusion | flops 545259520 | bytes 34668544 | tf_op jit(solution)/shard_map/dot_general | solution.py:78
  54.7 137.0 %all-reduce.12.cloned.1.call-done = (f32[32,32,512]{2,0,1:T(8,128)}, f32[32,512]{1,0:T(8,128)}) async-done(((f32[32,32,512]{2,0,1:T(8,128)}, f32[32,512]{1,0:T(8,128)}), (f32[32,32,512]{2,0,1:T(8,128)}, f32[32,512]{1,0:T(8,128)})) %all-reduce.12.cloned.1.call-update) | async-done | bytes 2162704 | tf_op jit(solution)/shard_map/psum | solution.py:100
  191.7 1.8 broadcast_add_fusion
  291.6 12.0 broadcast_in_dim.635
  303.5 15.2 bitcast_select_fusion
  318.8 8.8 fusion.224
  327.6 1.9 copy-done.5
  329.5 3.4 convolution_bitcast_fusion.2
  332.9 39.6 %psum.37 = f32[64,64,1]{1,0,2:T(8,128)S(1)} all-reduce(f32[64,64,1]{1,0,2:T(8,128)S(1)} %convolution_bitcast_fusion.2), channel_id=1, replica_groups=mesh['rows'=8,'sub'=4] {'rows','sub'}, use_global_device_ids=true, to_apply=%region_97.98 | all-reduce | flops 4096 | bytes 32768 | tf_op jit(solution)/shard_map/psum | solution.py:116
  510.2 1.4 fusion.497
  516.1 1.4 fusion.493
  530.4 1.4 fusion.483
  566.0 1.4 fusion.458
  578.8 1.4 fusion.449
  581.6 6.0 convolution_convert_fusion.2
  587.6 8.8 fusion.526
  596.5 133.4 %reduce-scatter.3.cloned.1.call-done = f32[16,64]{1,0:T(8,128)} async-done(((f32[512,64]{1,0:T(8,128)}), f32[16,64]{1,0:T(8,128)}) %reduce-scatter.3.cloned.1.call-update) | async-done | bytes 4112 | tf_op jit(solution)/shard_map/reduce_scatter | solution.py:120
  730.6 64.8 %all_gather.6 = bf16[512,64]{1,0:T(8,128)(2,1)S(1)} all-gather(bf16[16,64]{1,0:T(8,128)(2,1)S(1)} %convert_element_type.415), channel_id=1, replica_groups=mesh['rows'=8,'sub'=4] {'rows','sub'}, dimensions={0}, use_global_device_ids=true | all-gather | bytes 67584 | tf_op jit(solution)/shard_map/all_gather | solution.py:123
  795.3 8.9 fusion.527
  804.2 1.9 copy-done.4
  806.2 3.4 convolution_bitcast_fusion.1
  809.6 39.9 %psum.38 = f32[64,64,1]{1,0,2:T(8,128)S(1)} all-reduce(f32[64,64,1]{1,0,2:T(8,128)S(1)} %convolution_bitcast_fusion.1), channel_id=1, replica_groups=mesh['rows'=8,'sub'=4] {'rows','sub'}, use_global_device_ids=true, to_apply=%region_226.227 | all-reduce | flops 4096 | bytes 32768 | tf_op jit(solution)/shard_map/psum | solution.py:116
  970.7 1.9 subtract_divide_fusion.3
  991.3 1.4 fusion.434
  1011.5 1.4 fusion.420
  1047.1 1.4 fusion.395
  1059.9 1.4 fusion.386
  1062.7 6.0 convolution_convert_fusion.1
  1068.7 8.8 fusion.528
  1077.5 133.0 %reduce-scatter.5.cloned.1.call-done = f32[16,64]{1,0:T(8,128)} async-done(((f32[512,64]{1,0:T(8,128)}), f32[16,64]{1,0:T(8,128)}) %reduce-scatter.5.cloned.1.call-update) | async-done | bytes 4112 | tf_op jit(solution)/shard_map/reduce_scatter | solution.py:120
  1211.2 64.8 %all_gather.7 = bf16[512,64]{1,0:T(8,128)(2,1)S(1)} all-gather(bf16[16,64]{1,0:T(8,128)(2,1)S(1)} %convert_element_type.417), channel_id=1, replica_groups=mesh['rows'=8,'sub'=4] {'rows','sub'}, dimensions={0}, use_global_device_ids=true | all-gather | bytes 67584 | tf_op jit(solution)/shard_map/all_gather | solution.py:123
  1276.0 8.9 fusion.529
  1284.9 1.9 copy-done.3
  1286.8 3.4 convolution_bitcast_fusion
  1290.2 39.9 %psum.39 = f32[64,64,1]{1,0,2:T(8,128)S(1)} all-reduce(f32[64,64,1]{1,0,2:T(8,128)S(1)} %convolution_bitcast_fusion), channel_id=1, replica_groups=mesh['rows'=8,'sub'=4] {'rows','sub'}, use_global_device_ids=true, to_apply=%region_355.356 | all-reduce | flops 4096 | bytes 32768 | tf_op jit(solution)/shard_map/psum | solution.py:116
  1450.6 1.9 subtract_divide_fusion.2
  1452.6 1.4 fusion.384
  1462.7 1.4 fusion.377
  1468.5 1.4 fusion.373
  1482.8 1.4 fusion.363
  1508.6 1.4 fusion.345
  1520.1 1.4 fusion.337
  1530.0 1.4 fusion.330
  1537.1 5.7 convolution_multiply_fusion
  (2318 shorter events, 565.0 us)
Async XLA Ops:
  7.2 1.3 copy-start
  7.2 184.5 %all-reduce.12.cloned.1.call-start = ((), (), s32[]{:S(2)}) async-start(), calls=%async_computation.4 | async-start | bytes 4325376 | tf_op jit(solution)/shard_map/psum | solution.py:100
  9.1 2.1 copy-start.8
  54.0 675.8 %reduce-scatter.3.cloned.1.call-start = ((), (), s32[]{:S(2)}) async-start(), calls=%async_computation.2 | async-start | bytes 270336 | tf_op jit(solution)/shard_map/reduce_scatter | solution.py:120
  54.7 443.3 %copy-start.9 = (f32[64,64]{1,0:T(8,128)}, f32[64,64]{1,0:T(8,128)S(1)}, u32[]{:S(2)}) copy-start(f32[64,64]{1,0:T(8,128)S(1)} %fusion.228) | copy-start | bytes 49156
  210.1 2.8 copy-start.2
  238.2 3.3 copy-start.6
  291.5 12.0 copy-start.7
  303.5 15.2 copy-start.10
  327.5 1.9 copy-start.5
  596.4 614.1 %reduce-scatter.5.cloned.1.call-start = ((), (), s32[]{:S(2)}) async-start(), calls=%async_computation.3 | async-start | bytes 270336 | tf_op jit(solution)/shard_map/reduce_scatter | solution.py:120
  804.2 1.9 copy-start.4
  1284.9 1.9 copy-start.3
  1537.0 5.7 copy-start.1
Sparse Core Ops, SparseCore 0:
  54.2 137.4 all-reduce.11
  596.5 133.2 reduce-scatter.2
  1077.6 132.8 reduce-scatter.4
where the time goes:
time: 1580 us; the launch traced here: 1550 us
  waiting for transfers between devices  403 us (26%)
  other arithmetic  392 us (25%)
  blocking collectives  249 us (16%)
  local copies, waits for them, and re-layouts  234 us (15%)
  between operations  155 us (10%)
  matrix products  115 us (7%)
    div x219, other arithmetic, lower_solve(): (target[column] - jnp.sum(factor[column] * result, axis=0)) / factor[colu...  267 us
    reduce_scatter x2, waiting for transfers between devices, per_device(): lax.psum_scatter(contract_rows(filled, ortho_rows), ('rows', 'sub'), scat...  266 us
    psum x1, waiting for transfers between devices, per_device(): gram_total, right_total = lax.psum((grams, right), ('rows', 'sub'))  137 us
    all_gather x2, blocking collectives, per_device(): mixer = lax.all_gather(mixer_share, ('rows', 'sub'), axis=0, tiled=True)  130 us
    psum x3, blocking collectives, per_device(): products = lax.psum(local_gram, ('rows', 'sub'))  119 us
    slice x192, local copies, waits for them, and re-layouts, cholesky_last(): diagonal_root = jnp.sqrt(remain[column])  113 us
    dot_general x3, matrix products, contract_rows(): lax.dot_general(former, latter, (((1,), (1,)), ((), ())), preferred_eleme...  42 us
    dot_general x4, matrix products, contract_first(): lax.dot_general(former, latter, (((0,), (0,)), ((), ())), preferred_eleme...  41.8 us
  transfers between devices with their start and end apart: 3, of which 3 were waited for; matrix products, arithmetic and copies ran while one was open for 0% of the time, Pallas kernels for 0%

commit v1 on v0

--- a/solution.py
+++ b/solution.py
@@ -113,7 +113,13 @@
             precision=highest,
             preferred_element_type=jnp.float32,
         )
-        products = lax.psum(local_gram, ("rows", "sub"))
+
+        def touch_rings_in(x_local, comm_axis, axis_key):
+            oldest = lax.psum(x_local, comm_axis)
+            t_next = lax.psum(oldest, axis_name=axis_key)
+            return t_next
+
+        products = touch_rings_in(local_gram, "sub", "rows")
         inverse = inverse_factor(products)
         if sweep_index < POWER:
             ortho_rows = jnp.dot(inverse, sketch, precision=highest).astype(jnp.bfloat16)

time: 1580 us -> 1570 us (level)
    psum x3 -> x6, blocking collectives: 119 us -> 121 us  [the longest x3 67.1 us: touch_rings_in(): t_next = lax.psum(oldest, axis_name=axis_key)]
where the time goes in v1:
time: 1570 us; the launch traced here: 1550 us
  waiting for transfers between devices  399 us (25%)
  other arithmetic  392 us (25%)
  blocking collectives  250 us (16%)
  local copies, waits for them, and re-layouts  234 us (15%)
  between operations  155 us (10%)
  matrix products  115 us (7%)
    div x219, other arithmetic, lower_solve(): (target[column] - jnp.sum(factor[column] * result, axis=0)) / factor[colu...  267 us
    reduce_scatter x2, waiting for transfers between devices, per_device(): lax.psum_scatter(contract_rows(filled, ortho_rows), ('rows', 'sub'), scat...  262 us
    psum x1, waiting for transfers between devices, per_device(): gram_total, right_total = lax.psum((grams, right), ('rows', 'sub'))  137 us
    all_gather x2, blocking collectives, per_device(): mixer = lax.all_gather(mixer_share, ('rows', 'sub'), axis=0, tiled=True)  129 us
    slice x192, local copies, waits for them, and re-layouts, cholesky_last(): diagonal_root = jnp.sqrt(remain[column])  113 us
    psum x3, blocking collectives, touch_rings_in(): t_next = lax.psum(oldest, axis_name=axis_key)  67.1 us
    psum x3, blocking collectives, touch_rings_in(): oldest = lax.psum(x_local, comm_axis)  53.8 us
    dot_general x3, matrix products, contract_rows(): lax.dot_general(former, latter, (((1,), (1,)), ((), ())), preferred_eleme...  42 us
  transfers between devices with their start and end apart: 3, of which 3 were waited for; matrix products, arithmetic and copies ran while one was open for 0% of the time, Pallas kernels for 0%

profile of v1, /device:TPU:0, one launch (start us, length us, event | category | flops | bytes accessed | tf_op | source)
XLA Modules:
  0.0 1545.8 jit_solution(12233515524636403577)
XLA Ops:
  9.1 2.1 copy.518
  11.2 2.8 fusion.6
  14.1 2.5 copy.519
  16.6 12.9 mul.4308
  29.5 24.4 %fusion.2 = f32[32,512]{1,0:T(8,128)} fusion(bf16[32,16384]{1,0:T(8,128)(2,1)S(1)} %copy-done, bf16[512,16384]{1,0:T(8,128)(2,1)} %param.965, bf16[64,8,128,128]{3,2,1,0:T(8,128)(2,1)} %bitcast.3919), kind=kOutput, calls=%fused_computation.40 | convolution fusion | flops 545259520 | bytes 34668544 | tf_op jit(solution)/shard_map/dot_general | solution.py:78
  54.7 137.0 %all-reduce.12.cloned.1.call-done = (f32[32,32,512]{2,0,1:T(8,128)}, f32[32,512]{1,0:T(8,128)}) async-done(((f32[32,32,512]{2,0,1:T(8,128)}, f32[32,512]{1,0:T(8,128)}), (f32[32,32,512]{2,0,1:T(8,128)}, f32[32,512]{1,0:T(8,128)})) %all-reduce.12.cloned.1.call-update) | async-done | bytes 2162704 | tf_op jit(solution)/shard_map/psum | solution.py:100
  191.7 1.8 broadcast_add_fusion
  291.6 12.0 broadcast_in_dim.635
  303.6 15.2 bitcast_select_fusion
  318.8 8.8 fusion.224
  327.6 1.9 copy-done.5
  329.5 3.4 fusion.526
  332.9 18.1 %psum.58 = f32[64,64]{1,0:T(8,128)S(1)} all-reduce(f32[64,64]{1,0:T(8,128)S(1)} %fusion.526), channel_id=1, replica_groups=mesh['rows'=8,'sub'=4] {'sub'}, use_global_device_ids=true, to_apply=%region_97.98 | all-reduce | flops 4096 | bytes 32768 | tf_op jit(solution)/shard_map/psum | solution.py:118
  351.0 22.4 %psum.59 = f32[64,64,1]{1,0,2:T(8,128)S(1)} all-reduce(f32[64,64,1]{1,0,2:T(8,128)S(1)} %bitcast.3954), channel_id=1, replica_groups=mesh['rows'=8,'sub'=4] {'rows'}, use_global_device_ids=true, to_apply=%region_98.99 | all-reduce | flops 4096 | bytes 32768 | tf_op jit(solution)/shard_map/psum | solution.py:119
  511.0 1.4 fusion.497
  531.1 1.4 fusion.483
  566.7 1.4 fusion.458
  579.5 1.4 fusion.449
  582.7 6.0 convolution_convert_fusion.2
  588.7 8.8 fusion.527
  597.6 130.8 %reduce-scatter.3.cloned.1.call-done = f32[16,64]{1,0:T(8,128)} async-done(((f32[512,64]{1,0:T(8,128)}), f32[16,64]{1,0:T(8,128)}) %reduce-scatter.3.cloned.1.call-update) | async-done | bytes 4112 | tf_op jit(solution)/shard_map/reduce_scatter | solution.py:126
  729.0 64.6 %all_gather.6 = bf16[512,64]{1,0:T(8,128)(2,1)S(1)} all-gather(bf16[16,64]{1,0:T(8,128)(2,1)S(1)} %convert_element_type.415), channel_id=1, replica_groups=mesh['rows'=8,'sub'=4] {'rows','sub'}, dimensions={0}, use_global_device_ids=true | all-gather | bytes 67584 | tf_op jit(solution)/shard_map/all_gather | solution.py:129
  793.6 8.9 fusion.528
  802.5 1.9 copy-done.4
  804.4 3.4 fusion.529
  807.8 17.8 %psum.60 = f32[64,64]{1,0:T(8,128)S(1)} all-reduce(f32[64,64]{1,0:T(8,128)S(1)} %fusion.529), channel_id=1, replica_groups=mesh['rows'=8,'sub'=4] {'sub'}, use_global_device_ids=true, to_apply=%region_227.228 | all-reduce | flops 4096 | bytes 32768 | tf_op jit(solution)/shard_map/psum | solution.py:118
  825.7 22.4 %psum.61 = f32[64,64,1]{1,0,2:T(8,128)S(1)} all-reduce(f32[64,64,1]{1,0,2:T(8,128)S(1)} %bitcast.3955), channel_id=1, replica_groups=mesh['rows'=8,'sub'=4] {'rows'}, use_global_device_ids=true, to_apply=%region_228.229 | all-reduce | flops 4096 | bytes 32768 | tf_op jit(solution)/shard_map/psum | solution.py:119
  968.8 1.9 subtract_divide_fusion.3
  989.5 1.4 fusion.434
  1009.6 1.4 fusion.420
  1045.3 1.4 fusion.395
  1058.0 1.4 fusion.386
  1061.3 6.0 convolution_convert_fusion.1
  1067.2 8.8 fusion.530
  1076.1 130.8 %reduce-scatter.5.cloned.1.call-done = f32[16,64]{1,0:T(8,128)} async-done(((f32[512,64]{1,0:T(8,128)}), f32[16,64]{1,0:T(8,128)}) %reduce-scatter.5.cloned.1.call-update) | async-done | bytes 4112 | tf_op jit(solution)/shard_map/reduce_scatter | solution.py:126
  1207.5 64.7 %all_gather.7 = bf16[512,64]{1,0:T(8,128)(2,1)S(1)} all-gather(bf16[16,64]{1,0:T(8,128)(2,1)S(1)} %convert_element_type.417), channel_id=1, replica_groups=mesh['rows'=8,'sub'=4] {'rows','sub'}, dimensions={0}, use_global_device_ids=true | all-gather | bytes 67584 | tf_op jit(solution)/shard_map/all_gather | solution.py:129
  1272.2 8.9 fusion.531
  1281.1 1.9 copy-done.3
  1283.0 3.4 fusion.532
  1286.4 17.8 %psum.62 = f32[64,64]{1,0:T(8,128)S(1)} all-reduce(f32[64,64]{1,0:T(8,128)S(1)} %fusion.532), channel_id=1, replica_groups=mesh['rows'=8,'sub'=4] {'sub'}, use_global_device_ids=true, to_apply=%region_357.358 | all-reduce | flops 4096 | bytes 32768 | tf_op jit(solution)/shard_map/psum | solution.py:118
  1304.3 22.4 %psum.63 = f32[64,64,1]{1,0,2:T(8,128)S(1)} all-reduce(f32[64,64,1]{1,0,2:T(8,128)S(1)} %bitcast.3956), channel_id=1, replica_groups=mesh['rows'=8,'sub'=4] {'rows'}, use_global_device_ids=true, to_apply=%region_358.359 | all-reduce | flops 4096 | bytes 32768 | tf_op jit(solution)/shard_map/psum | solution.py:119
  1446.8 1.9 subtract_divide_fusion.2
  1448.8 1.4 fusion.384
  1459.0 1.4 fusion.377
  1464.7 1.4 fusion.373
  1516.3 1.4 fusion.337
  1526.3 1.4 fusion.330
  1533.3 5.7 convolution_multiply_fusion
  (2321 shorter events, 569.0 us)
Async XLA Ops:
  7.2 1.3 copy-start
  7.2 184.5 %all-reduce.12.cloned.1.call-start = ((), (), s32[]{:S(2)}) async-start(), calls=%async_computation.4 | async-start | bytes 4325376 | tf_op jit(solution)/shard_map/psum | solution.py:100
  9.1 2.1 copy-start.8
  54.0 674.3 %reduce-scatter.3.cloned.1.call-start = ((), (), s32[]{:S(2)}) async-start(), calls=%async_computation.2 | async-start | bytes 270336 | tf_op jit(solution)/shard_map/reduce_scatter | solution.py:126
  54.6 444.1 %copy-start.9 = (f32[64,64]{1,0:T(8,128)}, f32[64,64]{1,0:T(8,128)S(1)}, u32[]{:S(2)}) copy-start(f32[64,64]{1,0:T(8,128)S(1)} %fusion.228) | copy-start | bytes 49156
  210.2 2.8 copy-start.2
  238.2 3.3 copy-start.6
  291.6 12.0 copy-start.7
  303.6 15.2 copy-start.10
  327.5 1.9 copy-start.5
  597.5 609.3 %reduce-scatter.5.cloned.1.call-start = ((), (), s32[]{:S(2)}) async-start(), calls=%async_computation.3 | async-start | bytes 270336 | tf_op jit(solution)/shard_map/reduce_scatter | solution.py:126
  802.5 1.9 copy-start.4
  1281.1 1.9 copy-start.3
  1533.3 5.7 copy-start.1
Sparse Core Ops, SparseCore 0:
  54.1 137.5 all-reduce.11
  597.6 130.6 reduce-scatter.2
  1076.2 130.5 reduce-scatter.4
